TPU v7x, 128 devices: a whole 4x4x4 slice. The times are simulated.
128 devices in a mesh: row: 32 (over y, z, core), col: 4 (over x).
Axes of the slice: x: 4, y: 4, z: 4, core: 2. Of those that a mesh axis runs over, the one named last changes fastest.
Arguments:
- matrix: float32 [16384, 16, 512], P('row', 'col'), may hold values from -200 to 200, as said below
Outputs:
- factored: float32 [16384, 16, 512], P('row', 'col')
- upper_rows: float32 [2, 512, 16, 512], P(None, 'row', 'col')
Inputs may be any that keep to these rules, and one draw needn't show every extreme that they name: `matrix`: Real-valued entries; every panel has full column rank.
All inputs are finite; a program needn't handle non-finite values.
Results may differ from a plain program's by a relative error of at most 0.0001.
Values sent between devices are 32-bit elements; how exact they have to be, the bound alone decides.
A program may use at most 128 MiB of HBM per device.

v0:
```python
import jax
import jax.numpy as jnp
from jax import lax
from jax.sharding import PartitionSpec as P

PANELS = 2


HIGH = lax.Precision.HIGHEST


def spread(value, axis, root):
    mine = lax.axis_index(axis) == root
    return lax.psum(jnp.where(mine, value, jnp.zeros_like(value)), axis)


def right_solve(lower, block):
    eye = jnp.eye(lower.shape[0], dtype=jnp.float32)
    inverse = lax.linalg.triangular_solve(lower, eye, left_side=True, lower=True)
    return jnp.dot(block, inverse.T, precision=HIGH)


def gram_of(block):
    return jnp.dot(block.T, block, precision=HIGH)


def on_device(matrix):
    work = matrix
    row_dev, blocks, width = matrix.shape
    half = width // 2
    n_row = lax.axis_size("row")
    n_col = lax.axis_size("col")
    my_col = lax.axis_index("col")
    my_row = lax.axis_index("row")
    share = width // n_row
    scale = jnp.sqrt(jnp.float32(row_dev * n_row))
    number = jnp.arange(blocks) * n_col + my_col
    pieces = []
    for k in range(PANELS):
        root = k % n_col
        slot = k // n_col
        owner = my_col == root
        panel = work[:, slot, :]
        first = panel[:, :half]
        second = panel[:, half:]
        lower_one = jnp.linalg.cholesky(lax.psum(gram_of(first), "row"))
        basis_one = right_solve(lower_one, first)
        inner = lax.psum(jnp.dot(basis_one.T, second, precision=HIGH), "row")
        rest = second - jnp.dot(basis_one, inner, precision=HIGH)
        lower_two = jnp.linalg.cholesky(lax.psum(gram_of(rest), "row"))
        basis_two = right_solve(lower_two, rest)
        local_basis = jnp.concatenate([basis_one, basis_two], axis=1)
        top = jnp.concatenate([lower_one.T, inner], axis=1)
        bottom = jnp.concatenate([jnp.zeros((half, half), jnp.float32), lower_two.T], axis=1)
        upper = jnp.concatenate([top, bottom], axis=0)
        basis = spread(local_basis, "col", root)
        keep = (number > k).astype(jnp.float32)
        terms = jnp.einsum("rk,rbc->kbc", basis, work, precision=HIGH) * keep[None, :, None]
        weights = lax.psum(terms, "row")
        mine = lax.dynamic_slice_in_dim(weights, my_row * share, share, 0)
        work = work - jnp.einsum("rk,kbc->rbc", basis, weights, precision=HIGH)
        work = work.at[:, slot, :].set(jnp.where(owner, basis * scale, work[:, slot, :]))
        upper_share = lax.dynamic_slice_in_dim(upper, my_row * share, share, 0)
        mine = mine.at[:, slot, :].set(jnp.where(owner, upper_share, mine[:, slot, :]))
        pieces.append(mine)
    return (work, jnp.stack(pieces, axis=0))


def solution(mesh):
    placed = (P("row", "col", None),)
    return jax.shard_map(
        on_device,
        mesh=mesh,
        in_specs=placed,
        out_specs=(P("row", "col", None), P(None, "row", "col", None)),
        check_vma=False,
    )
```

profile of v0, /device:TPU:1, one launch (start us, length us, event | category | flops | bytes accessed | tf_op | source)
XLA Modules:
  0.0 1277.8 jit_solution(5746735367781790815)
XLA Ops:
  12.0 105.9 %all-reduce.14.cloned.1.call-done = f32[256,256]{0,1:T(8,128)} async-done(((f32[256,256]{0,1:T(8,128)}), f32[256,256]{0,1:T(8,128)}) %all-reduce.14.cloned.1.call-update) | async-done | bytes 262160 | tf_op jit(solution)/shard_map/psum | solution.py:46
  120.0 11.7 cholesky.214
  142.0 11.7 cholesky.231
  160.3 19.7 %custom-call.18 = f32[2,128,128]{1,2,0:T(8,128)S(1)} custom-call(f32[2,128,128]{2,1,0:T(8,128)S(1)} %get-tuple-element.78), custom_call_target="InvertDiagBlocksLowerTriangular" | custom-call | tf_op jit(solution)/shard_map/triangular_solve/custom-call.0 | solution.py:19
  183.3 102.1 %all-reduce.16.cloned.1.call-done = f32[256,256]{0,1:T(8,128)} async-done(((f32[256,256]{0,1:T(8,128)}), f32[256,256]{0,1:T(8,128)}) %all-reduce.16.cloned.1.call-update) | async-done | bytes 262160 | tf_op jit(solution)/shard_map/psum | solution.py:48
  289.6 101.7 %all-reduce.18.cloned.1.call-done = f32[256,256]{0,1:T(8,128)} async-done(((f32[256,256]{0,1:T(8,128)}), f32[256,256]{0,1:T(8,128)}) %all-reduce.18.cloned.1.call-update) | async-done | bytes 262160 | tf_op jit(solution)/shard_map/psum | solution.py:50
  393.4 11.7 cholesky.248
  415.6 11.7 cholesky.265
  434.4 19.7 %custom-call.20 = f32[2,128,128]{1,2,0:T(8,128)S(1)} custom-call(f32[2,128,128]{2,1,0:T(8,128)S(1)} %get-tuple-element.79), custom_call_target="InvertDiagBlocksLowerTriangular" | custom-call | tf_op jit(solution)/shard_map/triangular_solve/custom-call.0 | solution.py:19
  462.1 38.5 %all-reduce.20.cloned.1.call-done = f32[512,512]{0,1:T(8,128)} async-done(((f32[512,512]{0,1:T(8,128)}), f32[512,512]{0,1:T(8,128)}) %all-reduce.20.cloned.1.call-update) | async-done | bytes 1048592 | tf_op jit(solution)/shard_map/psum | solution.py:14
  510.8 114.6 %all-reduce.22.cloned.1.call-done = f32[512,4,512]{0,2,1:T(8,128)} async-done(((f32[512,4,512]{0,2,1:T(8,128)}), f32[512,4,512]{0,2,1:T(8,128)}) %all-reduce.22.cloned.1.call-update) | async-done | bytes 4194320 | tf_op jit(solution)/shard_map/psum | solution.py:59
  638.7 101.8 %all-reduce.24.cloned.1.call-done = f32[256,256]{0,1:T(8,128)} async-done(((f32[256,256]{0,1:T(8,128)}), f32[256,256]{0,1:T(8,128)}) %all-reduce.24.cloned.1.call-update) | async-done | bytes 262160 | tf_op jit(solution)/shard_map/psum | solution.py:46
  742.5 11.7 cholesky.282
  764.6 11.7 cholesky.299
  783.5 19.7 %custom-call.22 = f32[2,128,128]{1,2,0:T(8,128)S(1)} custom-call(f32[2,128,128]{2,1,0:T(8,128)S(1)} %get-tuple-element.80), custom_call_target="InvertDiagBlocksLowerTriangular" | custom-call | tf_op jit(solution)/shard_map/triangular_solve/custom-call.0 | solution.py:19
  806.1 102.1 %all-reduce.26.cloned.1.call-done = f32[256,256]{0,1:T(8,128)} async-done(((f32[256,256]{0,1:T(8,128)}), f32[256,256]{0,1:T(8,128)}) %all-reduce.26.cloned.1.call-update) | async-done | bytes 262160 | tf_op jit(solution)/shard_map/psum | solution.py:48
  911.4 102.1 %all-reduce.28.cloned.1.call-done = f32[256,256]{0,1:T(8,128)} async-done(((f32[256,256]{0,1:T(8,128)}), f32[256,256]{0,1:T(8,128)}) %all-reduce.28.cloned.1.call-update) | async-done | bytes 262160 | tf_op jit(solution)/shard_map/psum | solution.py:50
  1015.5 11.7 cholesky.316
  1037.8 11.7 cholesky.333
  1057.0 19.7 %custom-call.24 = f32[2,128,128]{1,2,0:T(8,128)S(1)} custom-call(f32[2,128,128]{2,1,0:T(8,128)S(1)} %get-tuple-element.81), custom_call_target="InvertDiagBlocksLowerTriangular" | custom-call | tf_op jit(solution)/shard_map/triangular_solve/custom-call.0 | solution.py:19
  1080.4 42.7 %all-reduce.30.cloned.1.call-done = f32[512,512]{0,1:T(8,128)} async-done(((f32[512,512]{0,1:T(8,128)}), f32[512,512]{0,1:T(8,128)}) %all-reduce.30.cloned.1.call-update) | async-done | bytes 1048592 | tf_op jit(solution)/shard_map/psum | solution.py:14
  1123.1 10.2 convolution_multiply_fusion
  1137.6 110.4 %all-reduce.32.cloned.1.call-done = f32[512,4,512]{0,2,1:T(8,128)} async-done(((f32[512,4,512]{0,2,1:T(8,128)}), f32[512,4,512]{0,2,1:T(8,128)}) %all-reduce.32.cloned.1.call-update) | async-done | bytes 4194320 | tf_op jit(solution)/shard_map/psum | solution.py:59
  1252.2 10.5 convolution_subtract_fusion
  (169 shorter events, 158.3 us)
Async XLA Ops:
  7.2 110.7 %all-reduce.14.cloned.1.call-start = ((), (), s32[]{:S(2)}) async-start(), calls=%async_computation | async-start | bytes 524288 | tf_op jit(solution)/shard_map/psum | solution.py:46
  11.9 273.5 %all-reduce.16.cloned.1.call-start = ((), (), s32[]{:S(2)}) async-start(), calls=%async_computation.1 | async-start | bytes 524288 | tf_op jit(solution)/shard_map/psum | solution.py:48
  183.3 208.0 %all-reduce.18.cloned.1.call-start = ((), (), s32[]{:S(2)}) async-start(), calls=%async_computation.2 | async-start | bytes 524288 | tf_op jit(solution)/shard_map/psum | solution.py:50
  289.1 211.4 %all-reduce.20.cloned.1.call-start = ((), (), s32[]{:S(2)}) async-start(), calls=%async_computation.3 | async-start | bytes 2097152 | tf_op jit(solution)/shard_map/psum | solution.py:14
  456.8 168.6 %all-reduce.22.cloned.1.call-start = ((), (), s32[]{:S(2)}) async-start(), calls=%async_computation.4 | async-start | bytes 8388608 | tf_op jit(solution)/shard_map/psum | solution.py:59
  510.7 114.7 %copy-start.2 = (f32[512,512]{0,1:T(8,128)S(1)}, f32[512,512]{0,1:T(8,128)}, u32[]{:S(2)}) copy-start(f32[512,512]{0,1:T(8,128)} %all-reduce.20.cloned.1.call-done) | copy-start | bytes 3145732
  510.7 229.7 %all-reduce.24.cloned.1.call-start = ((), (), s32[]{:S(2)}) async-start(), calls=%async_computation.5 | async-start | bytes 524288 | tf_op jit(solution)/shard_map/psum | solution.py:46
  634.6 2.0 copy-start
  638.2 270.0 %all-reduce.26.cloned.1.call-start = ((), (), s32[]{:S(2)}) async-start(), calls=%async_computation.6 | async-start | bytes 524288 | tf_op jit(solution)/shard_map/psum | solution.py:48
  806.1 207.4 %all-reduce.28.cloned.1.call-start = ((), (), s32[]{:S(2)}) async-start(), calls=%async_computation.7 | async-start | bytes 524288 | tf_op jit(solution)/shard_map/psum | solution.py:50
  911.2 212.0 %all-reduce.30.cloned.1.call-start = ((), (), s32[]{:S(2)}) async-start(), calls=%async_computation.8 | async-start | bytes 2097152 | tf_op jit(solution)/shard_map/psum | solution.py:14
  1079.3 168.7 %all-reduce.32.cloned.1.call-start = ((), (), s32[]{:S(2)}) async-start(), calls=%async_computation.9 | async-start | bytes 8388608 | tf_op jit(solution)/shard_map/psum | solution.py:59
  1133.3 0.9 copy-start.3
  1133.3 114.7 %copy-start.4 = (f32[256,256]{0,1:T(8,128)S(1)}, f32[256,256]{0,1:T(8,128)}, u32[]{:S(2)}) copy-start(f32[256,256]{0,1:T(8,128)} %all-reduce.26.cloned.1.call-done) | copy-start | bytes 786436
  1133.3 114.7 %copy-start.5 = (f32[256,256]{0,1:T(8,128)S(1)}, f32[256,256]{0,1:T(8,128)}, u32[]{:S(2)}) copy-start(f32[256,256]{0,1:T(8,128)} %get-tuple-element.132) | copy-start | bytes 786436
  1133.3 114.7 %copy-start.6 = (f32[256,256]{0,1:T(8,128)S(1)}, f32[256,256]{0,1:T(8,128)}, u32[]{:S(2)}) copy-start(f32[256,256]{0,1:T(8,128)} %get-tuple-element.130) | copy-start | bytes 786436
  1135.6 116.6 %copy-start.1 = (f32[512,512]{0,1:T(8,128)S(1)}, f32[512,512]{0,1:T(8,128)}, u32[]{:S(2)}) copy-start(f32[512,512]{0,1:T(8,128)} %all-reduce.30.cloned.1.call-done) | copy-start | bytes 3145732
Sparse Core Ops, SparseCore 0:
  12.0 105.7 all-reduce.13
  183.4 102.0 all-reduce.15
  289.3 101.9 all-reduce.17
  456.9 43.6 all-reduce.19
  510.9 114.5 all-reduce.21
  638.4 102.0 all-reduce.23
  806.2 101.9 all-reduce.25
  911.4 101.9 all-reduce.27
  1079.4 43.6 all-reduce.29
  1133.5 114.5 all-reduce.31
where the time goes:
time: 1290 us; the launch traced here: 1280 us
  waiting for transfers between devices  922 us (71%)
  other arithmetic  229 us (18%)
  matrix products  60.8 us (5%)
  local copies, waits for them, and re-layouts  43 us (3%)
  between operations  20.3 us (2%)
    psum x2, waiting for transfers between devices, on_device(): weights = lax.psum(terms, 'row')  225 us
    psum x2, waiting for transfers between devices, on_device(): lower_one = jnp.linalg.cholesky(lax.psum(gram_of(first), 'row'))  208 us
    psum x2, waiting for transfers between devices, on_device(): inner = lax.psum(jnp.dot(basis_one.T, second, precision=HIGH), 'row')  204 us
    psum x2, waiting for transfers between devices, on_device(): lower_two = jnp.linalg.cholesky(lax.psum(gram_of(rest), 'row'))  204 us
    psum x2, waiting for transfers between devices, spread(): return lax.psum(jnp.where(mine, value, jnp.zeros_like(value)), axis)  81.2 us
    another operation x5, other arithmetic, right_solve(): lax.linalg.triangular_solve(lower, eye, left_side=True, lower=True)  78.7 us
    another operation x14, other arithmetic, on_device(): lower_two = jnp.linalg.cholesky(lax.psum(gram_of(rest), 'row'))  69.3 us
    another operation x13, other arithmetic, on_device(): lower_one = jnp.linalg.cholesky(lax.psum(gram_of(first), 'row'))  68.6 us
  transfers between devices with their start and end apart: 10, of which 10 were waited for; matrix products, arithmetic and copies ran while one was open for 1% of the time, Pallas kernels for 0%

commit v1 on v0

v1 whole, which is shorter than its diff:
```python
import jax
import jax.numpy as jnp
from jax import lax
from jax.sharding import PartitionSpec as P

PANELS = 2
HIGHEST = lax.Precision.HIGHEST
HIGH = lax.Precision.HIGH


def spread(value, axis, root):
    mine = lax.axis_index(axis) == root
    return lax.psum(jnp.where(mine, value, jnp.zeros_like(value)), axis)


def on_device(matrix):
    work = matrix
    row_dev, blocks, width = matrix.shape
    n_row = lax.axis_size("row")
    n_col = lax.axis_size("col")
    my_col = lax.axis_index("col")
    my_row = lax.axis_index("row")
    share = width // n_row
    scale = jnp.sqrt(jnp.float32(row_dev * n_row))
    number = jnp.arange(blocks) * n_col + my_col
    pieces = []
    for k in range(PANELS):
        root = k % n_col
        slot = k // n_col
        owner = my_col == root
        panel = spread(work[:, slot, :], "col", root)
        keep = (number > k).astype(jnp.float32)
        gram = jnp.dot(panel.T, panel, precision=HIGHEST)
        terms = jnp.einsum("rk,rbc->kbc", panel, work, precision=HIGH) * keep[None, :, None]
        both = lax.psum(jnp.concatenate([gram[:, None, :], terms], axis=1), "row")
        gram, terms = both[:, 0, :], both[:, 1:, :]
        lower = jnp.linalg.cholesky(gram)
        eye = jnp.eye(width, dtype=jnp.float32)
        inverse = lax.linalg.triangular_solve(lower, eye, left_side=True, lower=True)
        basis = jnp.dot(panel, inverse.T, precision=HIGHEST)
        weights = jnp.einsum("ij,jbc->ibc", inverse, terms, precision=HIGH)
        work = work - jnp.einsum("rk,kbc->rbc", basis, weights, precision=HIGH)
        work = work.at[:, slot, :].set(jnp.where(owner, basis * scale, work[:, slot, :]))
        mine = lax.dynamic_slice_in_dim(weights, my_row * share, share, 0)
        upper_share = lax.dynamic_slice_in_dim(lower.T, my_row * share, share, 0)
        mine = mine.at[:, slot, :].set(jnp.where(owner, upper_share, mine[:, slot, :]))
        pieces.append(mine)
    return (work, jnp.stack(pieces, axis=0))


def solution(mesh):
    placed = (P("row", "col", None),)
    return jax.shard_map(
        on_device,
        mesh=mesh,
        in_specs=placed,
        out_specs=(P("row", "col", None), P(None, "row", "col", None)),
        check_vma=False,
    )
```

time: 1290 us -> 706 us (0.55)
  waiting for transfers between devices: 922 us -> 319 us
  other arithmetic: 229 us -> 259 us
    psum x8 -> x2, waiting for transfers between devices: 841 us -> 229 us  [on_device(): both = lax.psum(jnp.concatenate([gram[:, None, :], terms], axis=1), 'row')]
    another operation x32 -> x34, other arithmetic: 217 us -> 244 us  [the longest x29 163 us: on_device(): lower = jnp.linalg.cholesky(gram)]
    dot_general x14 -> x8, matrix products: 35.4 us -> 38.7 us  [the longest x2 13.6 us: on_device(): weights = jnp.einsum('ij,jbc->ibc', inverse, terms, precision=HIGH)]
  transfers between devices with their start and end apart: 10 -> 4, of which waited for: 10 -> 4; matrix products, arithmetic and copies ran while one was open for 1% -> 1% of each run, Pallas kernels for 0% -> 0%
where the time goes in v1:
time: 706 us; the launch traced here: 701 us
  waiting for transfers between devices  319 us (45%)
  other arithmetic  259 us (37%)
  matrix products  60.1 us (9%)
  local copies, waits for them, and re-layouts  42.1 us (6%)
  between operations  19.8 us (3%)
    psum x2, waiting for transfers between devices, on_device(): both = lax.psum(jnp.concatenate([gram[:, None, :], terms], axis=1), 'row')  229 us
    another operation x29, other arithmetic, on_device(): lower = jnp.linalg.cholesky(gram)  163 us
    psum x2, waiting for transfers between devices, spread(): return lax.psum(jnp.where(mine, value, jnp.zeros_like(value)), axis)  90.3 us
    another operation x5, other arithmetic, on_device(): lax.linalg.triangular_solve(lower, eye, left_side=True, lower=True)  81.2 us
    another operation x27, local copies, waits for them, and re-layouts, on_device(): lax.linalg.triangular_solve(lower, eye, left_side=True, lower=True)  16 us
  transfers between devices with their start and end apart: 4, of which 4 were waited for; matrix products, arithmetic and copies ran while one was open for 1% of the time, Pallas kernels for 0%

profile of v1, /device:TPU:1, one launch (start us, length us, event | category | flops | bytes accessed | tf_op | source)
XLA Modules:
  0.0 700.6 jit_solution(209174848330328318)
XLA Ops:
  12.6 47.5 %all-reduce.6.cloned.1.call-done = f32[512,512]{0,1:T(8,128)} async-done(((f32[512,512]{0,1:T(8,128)}), f32[512,512]{0,1:T(8,128)}) %all-reduce.6.cloned.1.call-update) | async-done | bytes 1048592 | tf_op jit(solution)/shard_map/psum | solution.py:13
  63.5 6.7 fusion.6
  73.5 116.3 %all-reduce.8.cloned.1.call-done = f32[512,5,512]{0,2,1:T(8,128)} async-done(((f32[512,5,512]{0,2,1:T(8,128)}), f32[512,5,512]{0,2,1:T(8,128)}) %all-reduce.8.cloned.1.call-update) | async-done | bytes 5242896 | tf_op jit(solution)/shard_map/psum | solution.py:35
  193.0 11.7 %cholesky.286 = f32[128,128]{1,0:T(8,128)S(1)} custom-call(f32[128,128]{1,0:T(8,128)S(1)} %cholesky.426), custom_call_target="Cholesky" | custom-call | tf_op jit(solution)/shard_map/jit(cholesky)/cholesky | solution.py:37
  205.3 9.8 %custom-call.27 = f32[1,128,128]{1,2,0:T(8,128)S(1)} custom-call(f32[1,128,128]{2,1,0:T(8,128)S(1)} %get-tuple-element.117), custom_call_target="InvertDiagBlocksLowerTriangular" | custom-call | tf_op jit(solution)/shard_map/jit(cholesky)/cholesky | solution.py:37
  217.8 13.2 %cholesky.305 = f32[128,128]{1,0:T(8,128)} custom-call(f32[128,128]{1,0:T(8,128)} %cholesky.430), custom_call_target="Cholesky" | custom-call | tf_op jit(solution)/shard_map/jit(cholesky)/cholesky | solution.py:37
  231.9 10.0 %custom-call.28 = f32[1,128,128]{1,2,0:T(8,128)S(1)} custom-call(f32[1,128,128]{2,1,0:T(8,128)S(1)} %get-tuple-element.114), custom_call_target="InvertDiagBlocksLowerTriangular" | custom-call | tf_op jit(solution)/shard_map/jit(cholesky)/cholesky | solution.py:37
  242.5 11.7 %cholesky.326 = f32[128,128]{1,0:T(8,128)S(1)} custom-call(f32[128,128]{1,0:T(8,128)S(1)} %cholesky.435), custom_call_target="Cholesky" | custom-call | tf_op jit(solution)/shard_map/jit(cholesky)/cholesky | solution.py:37
  255.0 9.8 %custom-call.29 = f32[1,128,128]{1,2,0:T(8,128)S(1)} custom-call(f32[1,128,128]{2,1,0:T(8,128)S(1)} %get-tuple-element.111), custom_call_target="InvertDiagBlocksLowerTriangular" | custom-call | tf_op jit(solution)/shard_map/jit(cholesky)/cholesky | solution.py:37
  265.4 12.1 %cholesky.343 = f32[128,128]{1,0:T(8,128)S(1)} custom-call(f32[128,128]{1,0:T(8,128)S(1)} %convolution_subtract_fusion.12), custom_call_target="Cholesky" | custom-call | tf_op jit(solution)/shard_map/jit(cholesky)/cholesky | solution.py:37
  282.7 8.0 %while.8 = (s32[]{:T(128)}, f32[512,512]{1,0:T(8,128)S(1)}, s32[4,2]{0,1:T(2,128)S(1)}, f32[4,128,128]{2,1,0:T(8,128)S(1)}, s32[]{:T(128)}) while((s32[]{:T(128)}, f32[512,512]{1,0:T(8,128)S(1)}, s32[4,2]{0,1:T(2,128)S(1)}, f32[4,128,128]{2,1,0:T(8,128)S(1)}, s32[]{:T(128)}) %tuple.74), condition=%wide.while_cond.4, body=%wide.while_body.4.sunk | while | flops 2 | bytes 131181 | solution.py:39
  290.7 39.3 %custom-call.30 = f32[4,128,128]{1,2,0:T(8,128)S(1)} custom-call(f32[4,128,128]{2,1,0:T(8,128)S(1)} %get-tuple-element.66), custom_call_target="InvertDiagBlocksLowerTriangular" | custom-call | tf_op jit(solution)/shard_map/triangular_solve/custom-call.3 | solution.py:39
  333.3 6.9 fusion.2
  352.4 42.8 %all-reduce.10.cloned.1.call-done = f32[512,512]{1,0:T(8,128)} async-done(((f32[512,512]{1,0:T(8,128)}), f32[512,512]{1,0:T(8,128)}) %all-reduce.10.cloned.1.call-update) | async-done | bytes 1048592 | tf_op jit(solution)/shard_map/psum | solution.py:13
  412.2 112.4 %all-reduce.12.cloned.1.call-done = f32[512,5,512]{0,2,1:T(8,128)} async-done(((f32[512,5,512]{0,2,1:T(8,128)}), f32[512,5,512]{0,2,1:T(8,128)}) %all-reduce.12.cloned.1.call-update) | async-done | bytes 5242896 | tf_op jit(solution)/shard_map/psum | solution.py:35
  527.6 11.7 %cholesky.358 = f32[128,128]{1,0:T(8,128)S(1)} custom-call(f32[128,128]{1,0:T(8,128)S(1)} %cholesky.439), custom_call_target="Cholesky" | custom-call | tf_op jit(solution)/shard_map/jit(cholesky)/cholesky | solution.py:37
  540.0 9.8 %custom-call.31 = f32[1,128,128]{1,2,0:T(8,128)S(1)} custom-call(f32[1,128,128]{2,1,0:T(8,128)S(1)} %get-tuple-element.107), custom_call_target="InvertDiagBlocksLowerTriangular" | custom-call | tf_op jit(solution)/shard_map/jit(cholesky)/cholesky | solution.py:37
  552.4 13.3 %cholesky.377 = f32[128,128]{1,0:T(8,128)} custom-call(f32[128,128]{1,0:T(8,128)} %cholesky.443), custom_call_target="Cholesky" | custom-call | tf_op jit(solution)/shard_map/jit(cholesky)/cholesky | solution.py:37
  568.0 9.8 %custom-call.32 = f32[1,128,128]{1,2,0:T(8,128)S(1)} custom-call(f32[1,128,128]{2,1,0:T(8,128)S(1)} %get-tuple-element.104), custom_call_target="InvertDiagBlocksLowerTriangular" | custom-call | tf_op jit(solution)/shard_map/jit(cholesky)/cholesky | solution.py:37
  578.5 11.7 %cholesky.398 = f32[128,128]{1,0:T(8,128)S(1)} custom-call(f32[128,128]{1,0:T(8,128)S(1)} %cholesky.448), custom_call_target="Cholesky" | custom-call | tf_op jit(solution)/shard_map/jit(cholesky)/cholesky | solution.py:37
  590.9 9.8 %custom-call.33 = f32[1,128,128]{1,2,0:T(8,128)S(1)} custom-call(f32[1,128,128]{2,1,0:T(8,128)S(1)} %get-tuple-element.101), custom_call_target="InvertDiagBlocksLowerTriangular" | custom-call | tf_op jit(solution)/shard_map/jit(cholesky)/cholesky | solution.py:37
  601.3 11.9 %cholesky.415 = f32[128,128]{1,0:T(8,128)S(1)} custom-call(f32[128,128]{1,0:T(8,128)S(1)} %convolution_subtract_fusion.11), custom_call_target="Cholesky" | custom-call | tf_op jit(solution)/shard_map/jit(cholesky)/cholesky | solution.py:37
  617.6 8.2 %while.9 = (s32[]{:T(128)}, f32[512,512]{1,0:T(8,128)S(1)}, s32[4,2]{0,1:T(2,128)S(1)}, f32[4,128,128]{2,1,0:T(8,128)S(1)}, s32[]{:T(128)}) while((s32[]{:T(128)}, f32[512,512]{1,0:T(8,128)S(1)}, s32[4,2]{0,1:T(2,128)S(1)}, f32[4,128,128]{2,1,0:T(8,128)S(1)}, s32[]{:T(128)}) %tuple.88), condition=%wide.while_cond.4.clone, body=%wide.while_body.4.clone.sunk | while | flops 2 | bytes 131181 | solution.py:39
  625.8 39.3 %custom-call.34 = f32[4,128,128]{1,2,0:T(8,128)S(1)} custom-call(f32[4,128,128]{2,1,0:T(8,128)S(1)} %get-tuple-element.67), custom_call_target="InvertDiagBlocksLowerTriangular" | custom-call | tf_op jit(solution)/shard_map/triangular_solve/custom-call.3 | solution.py:39
  (149 shorter events, 113.0 us)
Async XLA Ops:
  7.2 52.9 %all-reduce.6.cloned.1.call-start = ((), (), s32[]{:S(2)}) async-start(), calls=%async_computation | async-start | bytes 2097152 | tf_op jit(solution)/shard_map/psum | solution.py:13
  12.5 177.3 %all-reduce.8.cloned.1.call-start = ((), (), s32[]{:S(2)}) async-start(), calls=%async_computation.1 | async-start | bytes 10485760 | tf_op jit(solution)/shard_map/psum | solution.py:35
  73.2 322.0 %all-reduce.10.cloned.1.call-start = ((), (), s32[]{:S(2)}) async-start(), calls=%async_computation.2 | async-start | bytes 2097152 | tf_op jit(solution)/shard_map/psum | solution.py:13
  204.7 0.6 copy-start.7
  333.2 6.9 copy-start.6
  333.2 10.4 %copy-start.2 = (f32[512,4,512]{2,1,0:T(4,128)S(1)}, f32[512,4,512]{2,1,0:T(4,128)}, u32[]{:S(2)}) copy-start(f32[512,4,512]{2,1,0:T(4,128)} %param.12) | copy-start | bytes 12582916
  340.2 7.7 %copy-start.3 = (f32[512,4,512]{2,0,1:T(8,128)}, f32[512,4,512]{2,0,1:T(8,128)S(1)}, u32[]{:S(2)}) copy-start(f32[512,4,512]{2,0,1:T(8,128)S(1)} %fusion.2) | copy-start | bytes 12582916
  347.9 2.0 copy-start
  351.3 173.3 %all-reduce.12.cloned.1.call-start = ((), (), s32[]{:S(2)}) async-start(), calls=%async_computation.3 | async-start | bytes 10485760 | tf_op jit(solution)/shard_map/psum | solution.py:35
  539.3 0.6 copy-start.8
  668.3 11.9 %copy-start.5 = (f32[512,512]{1,0:T(8,128)S(1)}, f32[512,512]{1,0:T(8,128)}, u32[]{:S(2)}) copy-start(f32[512,512]{1,0:T(8,128)} %all-reduce.10.cloned.1.call-done) | copy-start | bytes 3145732
  674.9 1.9 copy-start.4
  678.2 3.8 copy-start.1
Sparse Core Ops, SparseCore 0:
  12.7 47.3 all-reduce.5
  73.3 116.5 all-reduce.7
  351.4 43.7 all-reduce.9
  408.0 116.4 all-reduce.11
